TPU v7x, 32 devices: a whole 2x2x4 slice. The times are simulated.
32 devices in a mesh: col: 4 (over y, x), row: 8 (over z, core).
Axes of the slice: x: 2, y: 2, z: 4, core: 2. Of those that a mesh axis runs over, the one named last changes fastest.
Arguments:
- data: bfloat16 [16384, 8192], P('row', 'col'), may hold values from -6 to 6
- column_scale: float32 [8192], P('col'), may hold values from 0.25 to 4
- keep_mask: int32 [16384, 8192], P('row', 'col'), may hold values 0 or 1
Outputs:
- band: float32 [8192, 3, 2048], P('col', None, 'row')
All inputs are finite; a program needn't handle non-finite values. No bound on the sum of `keep_mask` on one device may be relied on, other than what follows from the above.
Results may differ from a plain program's by a relative error of at most 0.0012.
Values may be sent and summed in bfloat16 or wider, within the bound.
No kernel may reach another device: no remote copies, remote signals or barrier semaphores. Data moves between devices by JAX's collectives and lax.ppermute only.
A program may use at most 128 MiB of HBM per device.

v0:
```python
import jax
import jax.numpy as jnp
from jax import lax
from jax.sharding import PartitionSpec as P


def passed_along(block, axis, distance):
    devices = range(lax.axis_size(axis))
    route = [((i - distance) % len(devices), i) for i in devices]
    return lax.ppermute(block, axis, route)


def product(left, right):
    return lax.dot_general(
        left, right, (((0,), (0,)), ((), ())), preferred_element_type=jnp.float32
    )


def on_device(data, column_scale, keep_mask):
    values = data.astype(jnp.float32) * column_scale[None, :]
    colsq = lax.psum(jnp.sum(values * values, axis=0), "row")
    total_rows = data.shape[0] * lax.axis_size("row")
    divisor = jnp.minimum(jnp.sqrt(colsq + 1.0), jnp.sqrt(jnp.float32(total_rows)))
    scaled = (keep_mask.astype(jnp.float32) * values / divisor[None, :]).astype(jnp.bfloat16)
    offsets = lax.axis_size("col") // 2 + 1
    panels = [scaled]
    current = scaled
    for offset in range(1, offsets):
        current = passed_along(current, "col", -1)
        panels.append(current)
    summed = []
    for other in panels:
        summed.append(
            lax.psum_scatter(product(scaled, other), "row", scatter_dimension=1, tiled=True)
        )
    return jnp.stack(summed, axis=1)


def solution(mesh):
    in_specs = (P("row", "col"), P("col"), P("row", "col"))
    out_specs = P("col", None, "row")
    return jax.shard_map(
        on_device, mesh=mesh, in_specs=in_specs, out_specs=out_specs, check_vma=False
    )
```

profile of v0, /device:TPU:0, one launch (start us, length us, event | category | flops | bytes accessed | tf_op | source)
XLA Modules:
  0.0 657.1 jit_solution(13507558130262342819)
XLA Ops:
  6.5 0.0 copy-start.1
  6.5 0.0 reduce-scatter.4.cloned.1.call-start
  6.5 5.6 multiply_reduce_fusion
  12.2 18.4 %psum.7 = f32[2048]{0:T(1024)S(1)} all-reduce(f32[2048]{0:T(1024)S(1)} %multiply_reduce_fusion), channel_id=1, replica_groups=mesh['col'=4,'row'=8] {'row'}, use_global_device_ids=true, to_apply=%region_1.0 | all-reduce | flops 2048 | bytes 16384 | tf_op jit(solution)/shard_map/psum | solution.py:21
  30.5 0.0 copy-done.1
  30.5 9.4 %divide_convert_fusion = bf16[2048,2048]{1,0:T(8,128)(2,1)S(1)} fusion(bf16[2048,2048]{1,0:T(8,128)(2,1)} %param.3, s32[2048,2048]{1,0:T(8,128)} %param.5, f32[2048]{0:T(1024)S(1)} %sqrt_minimum_fusion, f32[2048]{0:T(1024)S(1)} %copy-done.1), kind=kLoop, calls=%fused_computation | loop fusion | flops 25165824 | bytes 33570816 | tf_op jit(solution)/shard_map/convert_element_type | solution.py:24
  40.0 0.0 copy-start
  40.0 3.2 copy-done
  43.2 21.0 %fusion = f32[2048,2048]{1,0:T(8,128)} fusion(bf16[2048,2048]{1,0:T(8,128)(2,1)S(1)} %divide_convert_fusion), kind=kOutput, calls=%fused_computation.5 | convolution fusion | flops 17179869184 | bytes 25165824 | tf_op jit(solution)/shard_map/dot_general | solution.py:14
  64.1 0.0 reduce-scatter.4.cloned.1.call-update
  64.1 0.0 reduce-scatter.6.cloned.1.call-start
  64.2 2.5 collective-permute-start
  66.7 177.2 %collective-permute-done = bf16[2048,2048]{1,0:T(8,128)(2,1)S(1)} collective-permute-done((bf16[2048,2048]{1,0:T(8,128)(2,1)}, bf16[2048,2048]{1,0:T(8,128)(2,1)S(1)}, u32[]{:S(2)}, u32[]{:S(2)}) %collective-permute-start) | collective-permute-done | bytes 8388640 | tf_op jit(solution)/shard_map/ppermute | solution.py:10
  243.9 0.0 copy-start.2
  243.9 3.2 copy-done.2
  247.1 22.6 %fusion.1 = f32[2048,2048]{1,0:T(8,128)} fusion(bf16[2048,2048]{1,0:T(8,128)(2,1)} %copy-done, bf16[2048,2048]{1,0:T(8,128)(2,1)S(1)} %collective-permute-done), kind=kOutput, calls=%fused_computation.6 | convolution fusion | flops 17179869184 | bytes 33554432 | tf_op jit(solution)/shard_map/dot_general | solution.py:14
  269.7 0.0 reduce-scatter.6.cloned.1.call-update
  269.7 0.0 reduce-scatter.8.cloned.1.call-start
  269.7 3.5 collective-permute-start.1
  273.2 176.3 %collective-permute-done.1 = bf16[2048,2048]{1,0:T(8,128)(2,1)S(1)} collective-permute-done((bf16[2048,2048]{1,0:T(8,128)(2,1)}, bf16[2048,2048]{1,0:T(8,128)(2,1)S(1)}, u32[]{:S(2)}, u32[]{:S(2)}) %collective-permute-start.1) | collective-permute-done | bytes 8388640 | tf_op jit(solution)/shard_map/ppermute | solution.py:10
  449.5 22.6 %fusion.2 = f32[2048,2048]{1,0:T(8,128)} fusion(bf16[2048,2048]{1,0:T(8,128)(2,1)} %copy-done, bf16[2048,2048]{1,0:T(8,128)(2,1)S(1)} %collective-permute-done.1), kind=kOutput, calls=%fused_computation.7 | convolution fusion | flops 17179869184 | bytes 33554432 | tf_op jit(solution)/shard_map/dot_general | solution.py:14
  472.1 0.0 reduce-scatter.8.cloned.1.call-update
  472.2 0.0 reduce-scatter.4.cloned.1.call-done
  472.2 0.0 reduce-scatter.6.cloned.1.call-done
  472.2 172.4 %reduce-scatter.8.cloned.1.call-done = f32[2048,256]{1,0:T(8,128)} async-done(((f32[2048,2048]{1,0:T(8,128)}), f32[2048,256]{1,0:T(8,128)}) %reduce-scatter.8.cloned.1.call-update) | async-done | bytes 2097168 | tf_op jit(solution)/shard_map/reduce_scatter | solution.py:34
  644.6 6.0 pad_maximum_fusion
  (1 shorter events, 0.0 us)
Async XLA Ops:
  6.5 24.0 %copy-start.1 = (f32[2048]{0:T(1024)S(1)}, f32[2048]{0:T(1024)}, u32[]{:S(2)}) copy-start(f32[2048]{0:T(1024)} %param.4) | copy-start | bytes 24580
  6.5 465.7 %reduce-scatter.4.cloned.1.call-start = ((), (), s32[]{:S(2)}) async-start(), calls=%async_computation.3 | async-start | bytes 18874368 | tf_op jit(solution)/shard_map/reduce_scatter | solution.py:34
  40.0 3.2 copy-start
  64.1 408.1 %reduce-scatter.6.cloned.1.call-start = ((), (), s32[]{:S(2)}) async-start(), calls=%async_computation.4 | async-start | bytes 18874368 | tf_op jit(solution)/shard_map/reduce_scatter | solution.py:34
  64.2 179.7 %collective-permute-start = (bf16[2048,2048]{1,0:T(8,128)(2,1)}, bf16[2048,2048]{1,0:T(8,128)(2,1)S(1)}, u32[]{:S(2)}, u32[]{:S(2)}) collective-permute-start(bf16[2048,2048]{1,0:T(8,128)(2,1)} %copy-done), channel_id=1, source_target_pairs={{8,0},{16,8},{24,16},{0,24},{9,1},{17,9},{25,17},{1,25},{10,2},{18... | collective-permute-start | bytes 25165832 | tf_op jit(solution)/shard_map/ppermute | solution.py:10
  243.9 3.2 copy-start.2
  269.7 374.9 %reduce-scatter.8.cloned.1.call-start = ((), (), s32[]{:S(2)}) async-start(), calls=%async_computation.5 | async-start | bytes 18874368 | tf_op jit(solution)/shard_map/reduce_scatter | solution.py:34
  269.7 179.8 %collective-permute-start.1 = (bf16[2048,2048]{1,0:T(8,128)(2,1)}, bf16[2048,2048]{1,0:T(8,128)(2,1)S(1)}, u32[]{:S(2)}, u32[]{:S(2)}) collective-permute-start(bf16[2048,2048]{1,0:T(8,128)(2,1)} %copy-done.2), channel_id=1, source_target_pairs={{8,0},{16,8},{24,16},{0,24},{9,1},{17,9},{25,17},{1,25},{10,2},{18... | collective-permute-start | bytes 25165832 | tf_op jit(solution)/shard_map/ppermute | solution.py:10
Sparse Core Ops, SparseCore 0:
  64.3 166.3 reduce-scatter.3
  269.8 168.0 reduce-scatter.5
  472.3 172.2 reduce-scatter.7
where the time goes:
time: 657 us
  waiting for transfers between devices  526 us (80%)
  matrix products  66.1 us (10%)
  other arithmetic  21 us (3%)
  blocking collectives  18.4 us (3%)
  between operations  13.2 us (2%)
    ppermute x2, waiting for transfers between devices, passed_along(): return lax.ppermute(block, axis, route)  353 us
    reduce_scatter x3, waiting for transfers between devices, on_device(): lax.psum_scatter(product(scaled, other), 'row', scatter_dimension=1, tile...  172 us
    dot_general x3, matrix products, product(): lax.dot_general(left, right, (((0,), (0,)), ((), ())), preferred_element_...  66.1 us
    psum x1, blocking collectives, on_device(): colsq = lax.psum(jnp.sum(values * values, axis=0), 'row')  18.4 us
  transfers between devices with their start and end apart: 5, of which 3 were waited for; matrix products, arithmetic and copies ran while one was open for 7% of the time, Pallas kernels for 0%

commit v1 on v0

--- a/solution.py
+++ b/solution.py
@@ -16,6 +16,39 @@
     )
 
 
+def reduced(partial, dimension, after):
+    if after is not None:
+        partial, _ = lax.optimization_barrier((partial, after))
+    return lax.psum_scatter(partial, "row", scatter_dimension=dimension, tiled=True)
+
+
+def mirrored(left, right, offset, after):
+    slots = lax.axis_size("row")
+    panels = lax.axis_size("col")
+    here = lax.axis_index("row")
+    width = left.shape[1] // slots
+    kept = slots // 2 + 1
+    wrapped = jnp.concatenate([left, left[:, : (kept - 1) * width]], axis=1)
+    partial = [
+        product(wrapped[:, r * width : (r + kept) * width], right[:, r * width : (r + 1) * width])
+        for r in range(slots)
+    ]
+    held = reduced(jnp.concatenate(partial, axis=0), 0, after)
+    blocks = [held]
+    for d in range(kept, slots):
+        e = slots - d
+        route = [
+            (((c + offset) % panels) * slots + (r + d) % slots, c * slots + r)
+            for c in range(panels)
+            for r in range(slots)
+        ]
+        sent = lax.ppermute(held[e * width : (e + 1) * width], ("col", "row"), route)
+        blocks.append(sent.T)
+    turned = jnp.concatenate(blocks, axis=0)
+    twice = jnp.concatenate([turned, turned], axis=0)
+    return lax.dynamic_slice_in_dim(twice, (slots - here) * width, slots * width, axis=0), held
+
+
 def on_device(data, column_scale, keep_mask):
     values = data.astype(jnp.float32) * column_scale[None, :]
     colsq = lax.psum(jnp.sum(values * values, axis=0), "row")
@@ -25,14 +58,18 @@
     offsets = lax.axis_size("col") // 2 + 1
     panels = [scaled]
     current = scaled
-    for offset in range(1, offsets):
+    for _ in range(1, offsets):
         current = passed_along(current, "col", -1)
         panels.append(current)
     summed = []
-    for other in panels:
-        summed.append(
-            lax.psum_scatter(product(scaled, other), "row", scatter_dimension=1, tiled=True)
-        )
+    last = None
+    for offset, other in enumerate(panels):
+        if (2 * offset) % lax.axis_size("col") == 0:
+            block, last = mirrored(scaled, other, offset, last)
+        else:
+            partial = product(scaled, other)
+            block = last = reduced(partial, 1, last)
+        summed.append(block)
     return jnp.stack(summed, axis=1)
 
 

time: 657 us -> 651 us (level)
  waiting for transfers between devices: 526 us -> 483 us
  matrix products: 66.1 us -> 86.4 us
  starting transfers between devices: 6.09 us -> 16.3 us
    reduce_scatter x3, waiting for transfers between devices: 172 us -> 89.5 us  [reduced(): lax.psum_scatter(partial, 'row', scatter_dimension=dimension, tiled=True)]
    ppermute x0 -> x6, waiting for transfers between devices: none -> 39.6 us  [mirrored(): sent = lax.ppermute(held[e * width:(e + 1) * width], ('col', 'row'), route)]
    dot_general x3 -> x17, matrix products: 66.1 us -> 86.4 us  [product(): lax.dot_general(left, right, (((0,), (0,)), ((), ())), preferred_element_...]
    ppermute x0 -> x6, starting transfers between devices: none -> 10.4 us  [mirrored(): sent = lax.ppermute(held[e * width:(e + 1) * width], ('col', 'row'), route)]
  transfers between devices with their start and end apart: 5 -> 11, of which waited for: 3 -> 8; matrix products, arithmetic and copies ran while one was open for 7% -> 9% of each run, Pallas kernels for 0% -> 0%
where the time goes in v1:
time: 651 us; the launch traced here: 647 us
  waiting for transfers between devices  483 us (74%)
  matrix products  86.4 us (13%)
  other arithmetic  18.5 us (3%)
  blocking collectives  18.4 us (3%)
  starting transfers between devices  16.3 us (3%)
  between operations  13.6 us (2%)
  local copies, waits for them, and re-layouts  11.5 us (2%)
    ppermute x2, waiting for transfers between devices, passed_along(): return lax.ppermute(block, axis, route)  353 us
    reduce_scatter x3, waiting for transfers between devices, reduced(): lax.psum_scatter(partial, 'row', scatter_dimension=dimension, tiled=True)  89.5 us
    dot_general x17, matrix products, product(): lax.dot_general(left, right, (((0,), (0,)), ((), ())), preferred_element_...  86.4 us
    ppermute x6, waiting for transfers between devices, mirrored(): sent = lax.ppermute(held[e * width:(e + 1) * width], ('col', 'row'), route)  39.6 us
    psum x1, blocking collectives, on_device(): colsq = lax.psum(jnp.sum(values * values, axis=0), 'row')  18.4 us
  transfers between devices with their start and end apart: 11, of which 8 were waited for; matrix products, arithmetic and copies ran while one was open for 9% of the time, Pallas kernels for 0%

profile of v1, /device:TPU:0, one launch (start us, length us, event | category | flops | bytes accessed | tf_op | source)
XLA Modules:
  0.0 647.4 jit_solution(359082656875674687)
XLA Ops:
  6.5 5.6 multiply_reduce_fusion
  12.2 18.4 %psum.7 = f32[2048]{0:T(1024)S(1)} all-reduce(f32[2048]{0:T(1024)S(1)} %multiply_reduce_fusion), channel_id=1, replica_groups=mesh['col'=4,'row'=8] {'row'}, use_global_device_ids=true, to_apply=%region_1.0 | all-reduce | flops 2048 | bytes 16384 | tf_op jit(solution)/shard_map/psum | solution.py:54
  30.5 9.8 %divide_convert_fusion = bf16[2048,2048]{1,0:T(8,128)(2,1)S(1)} fusion(bf16[2048,2048]{1,0:T(8,128)(2,1)} %param.3, s32[2048,2048]{1,0:T(8,128)} %param.5, f32[2048]{0:T(1024)S(1)} %sqrt_minimum_fusion, f32[2048]{0:T(1024)S(1)} %copy-done.5), kind=kLoop, calls=%fused_computation.3 | loop fusion | flops 25165824 | bytes 33570816 | tf_op jit(solution)/shard_map/convert_element_type | solution.py:57
  40.4 3.3 fusion.19
  44.3 2.7 fusion.25
  46.9 2.7 fusion.31
  49.6 2.7 fusion.37
  52.3 2.7 convolution_dynamic-update-slice_fusion.7
  55.0 2.7 convolution_dynamic-update-slice_fusion.6
  57.6 2.7 convolution_dynamic-update-slice_fusion.5
  60.4 14.9 %convolution_dynamic-update-slice_fusion.4 = f32[10240,256]{1,0:T(8,128)} fusion(f32[10240,256]{1,0:T(8,128)} %convolution_dynamic-update-slice_fusion.5, bf16[2048,2048]{1,0:T(8,128)(2,1)S(1)} %divide_convert_fusion, bf16[2048,1024]{1,0:T(8,128)(2,1)S(1)} %slice.141), kind=kOutput, calls=%fused_computation.34 | convolution fusion | flops 1352663040 | bytes 14942208 | tf_op jit(solution)/shard_map/dot_general | solution.py:14
  75.4 2.5 collective-permute-start.3
  77.9 177.2 %collective-permute-done.3 = bf16[2048,2048]{1,0:T(8,128)(2,1)S(1)} collective-permute-done((bf16[2048,2048]{1,0:T(8,128)(2,1)}, bf16[2048,2048]{1,0:T(8,128)(2,1)S(1)}, u32[]{:S(2)}, u32[]{:S(2)}) %collective-permute-start.3) | collective-permute-done | bytes 8388640 | tf_op jit(solution)/shard_map/ppermute | solution.py:10
  255.1 3.3 copy-done.6
  258.4 22.6 %fusion.67 = f32[2048,2048]{1,0:T(8,128)} fusion(bf16[2048,2048]{1,0:T(8,128)(2,1)} %copy-done, bf16[2048,2048]{1,0:T(8,128)(2,1)S(1)} %collective-permute-done.3), kind=kOutput, calls=%fused_computation.83 | convolution fusion | flops 17179869184 | bytes 33554432 | tf_op jit(solution)/shard_map/dot_general | solution.py:14
  281.1 3.3 collective-permute-start.4
  284.4 176.3 %collective-permute-done.4 = bf16[2048,2048]{1,0:T(8,128)(2,1)S(1)} collective-permute-done((bf16[2048,2048]{1,0:T(8,128)(2,1)}, bf16[2048,2048]{1,0:T(8,128)(2,1)S(1)}, u32[]{:S(2)}, u32[]{:S(2)}) %collective-permute-start.4) | collective-permute-done | bytes 8388640 | tf_op jit(solution)/shard_map/ppermute | solution.py:10
  460.7 5.1 fusion.22
  465.8 5.3 fusion.28
  471.1 5.3 fusion.34
  476.4 2.7 fusion.40
  479.1 2.7 convolution_dynamic-update-slice_fusion.3
  481.9 2.7 convolution_dynamic-update-slice_fusion.2
  484.6 2.8 convolution_dynamic-update-slice_fusion.1
  487.4 2.9 convolution_dynamic-update-slice_fusion
  493.0 5.1 collective-permute-start.2
  498.3 8.5 %collective-permute-done = f32[256,256]{0,1:T(8,128)S(1)} collective-permute-done((f32[256,256]{0,1:T(8,128)S(1)}, f32[256,256]{0,1:T(8,128)S(1)}, u32[]{:S(2)}, u32[]{:S(2)}) %collective-permute-start) | collective-permute-done | bytes 262176 | tf_op jit(solution)/shard_map/ppermute | solution.py:45
  506.8 9.3 %collective-permute-done.1 = f32[256,256]{0,1:T(8,128)S(1)} collective-permute-done((f32[256,256]{0,1:T(8,128)S(1)}, f32[256,256]{0,1:T(8,128)S(1)}, u32[]{:S(2)}, u32[]{:S(2)}) %collective-permute-start.1) | collective-permute-done | bytes 262176 | tf_op jit(solution)/shard_map/ppermute | solution.py:45
  516.1 6.1 collective-permute-done.2
  522.6 89.5 %reduce-scatter.8.cloned.1.call-done = f32[1280,256]{1,0:T(8,128)} async-done(((f32[10240,256]{1,0:T(8,128)}), f32[1280,256]{1,0:T(8,128)}) %reduce-scatter.8.cloned.1.call-update) | async-done | bytes 1310736 | tf_op jit(solution)/shard_map/reduce_scatter | solution.py:22
  620.0 14.4 %collective-permute-done.5 = f32[256,256]{0,1:T(8,128)S(1)} collective-permute-done((f32[256,256]{0,1:T(8,128)S(1)}, f32[256,256]{0,1:T(8,128)S(1)}, u32[]{:S(2)}, u32[]{:S(2)}) %collective-permute-start.5) | collective-permute-done | bytes 262176 | tf_op jit(solution)/shard_map/ppermute | solution.py:45
  637.5 3.1 pad_maximum_fusion
  (61 shorter events, 14.9 us)
Async XLA Ops:
  6.5 24.0 %copy-start.5 = (f32[2048]{0:T(1024)S(1)}, f32[2048]{0:T(1024)}, u32[]{:S(2)}) copy-start(f32[2048]{0:T(1024)} %param.4) | copy-start | bytes 24580
  6.5 274.4 %reduce-scatter.4.cloned.1.call-start = ((), (), s32[]{:S(2)}) async-start(), calls=%async_computation.3 | async-start | bytes 11796480 | tf_op jit(solution)/shard_map/reduce_scatter | solution.py:22
  40.3 20.0 %copy-start = (bf16[2048,2048]{1,0:T(8,128)(2,1)}, bf16[2048,2048]{1,0:T(8,128)(2,1)S(1)}, u32[]{:S(2)}) copy-start(bf16[2048,2048]{1,0:T(8,128)(2,1)S(1)} %divide_convert_fusion) | copy-start | bytes 25165828
  44.3 16.1 %copy-start.2 = (bf16[2048,1024]{1,0:T(8,128)(2,1)}, bf16[2048,1024]{1,0:T(8,128)(2,1)S(1)}, u32[]{:S(2)}) copy-start(bf16[2048,1024]{1,0:T(8,128)(2,1)S(1)} %slice.141) | copy-start | bytes 12582916
  75.3 414.9 %reduce-scatter.6.cloned.1.call-start = ((), (), s32[]{:S(2)}) async-start(), calls=%async_computation.4 | async-start | bytes 18874368 | tf_op jit(solution)/shard_map/reduce_scatter | solution.py:22
  75.4 179.7 %collective-permute-start.3 = (bf16[2048,2048]{1,0:T(8,128)(2,1)}, bf16[2048,2048]{1,0:T(8,128)(2,1)S(1)}, u32[]{:S(2)}, u32[]{:S(2)}) collective-permute-start(bf16[2048,2048]{1,0:T(8,128)(2,1)} %copy-done), channel_id=1, source_target_pairs={{8,0},{16,8},{24,16},{0,24},{9,1},{17,9},{25,17},{1,25},{10,2},{18... | collective-permute-start | bytes 25165832 | tf_op jit(solution)/shard_map/ppermute | solution.py:10
  255.1 3.4 copy-start.6
  281.0 331.1 %reduce-scatter.8.cloned.1.call-start = ((), (), s32[]{:S(2)}) async-start(), calls=%async_computation.5 | async-start | bytes 11796480 | tf_op jit(solution)/shard_map/reduce_scatter | solution.py:22
  281.1 179.6 %collective-permute-start.4 = (bf16[2048,2048]{1,0:T(8,128)(2,1)}, bf16[2048,2048]{1,0:T(8,128)(2,1)S(1)}, u32[]{:S(2)}, u32[]{:S(2)}) collective-permute-start(bf16[2048,2048]{1,0:T(8,128)(2,1)} %copy-done.6), channel_id=1, source_target_pairs={{8,0},{16,8},{24,16},{0,24},{9,1},{17,9},{25,17},{1,25},{10,2},{18... | collective-permute-start | bytes 25165832 | tf_op jit(solution)/shard_map/ppermute | solution.py:10
  465.8 10.6 %slice-start = ((s8[8388608]{0:T(1024)(128)(4,1)}), s8[4194304]{0:T(1024)(128)(4,1)S(1)}, s32[]{:S(2)}) async-start(s8[8388608]{0:T(1024)(128)(4,1)} %bitcast.25), calls=%async_computation.6 | async-start | bytes 8388608
  471.1 5.3 slice-start.1
  476.4 2.7 copy-start.3
  490.3 1.3 copy-start.1
  491.8 15.0 %collective-permute-start = (f32[256,256]{0,1:T(8,128)S(1)}, f32[256,256]{0,1:T(8,128)S(1)}, u32[]{:S(2)}, u32[]{:S(2)}) collective-permute-start(f32[256,256]{0,1:T(8,128)S(1)} %copy.10), channel_id=1, source_target_pairs={{5,0},{6,1},{7,2},{0,3},{1,4},{2,5},{3,6},{4,7},{13,8},{14,9},{15,... | collective-permute-start | bytes 786440 | tf_op jit(solution)/shard_map/ppermute | solution.py:45
  492.0 24.1 %collective-permute-start.1 = (f32[256,256]{0,1:T(8,128)S(1)}, f32[256,256]{0,1:T(8,128)S(1)}, u32[]{:S(2)}, u32[]{:S(2)}) collective-permute-start(f32[256,256]{0,1:T(8,128)S(1)} %copy.11), channel_id=1, source_target_pairs={{6,0},{7,1},{0,2},{1,3},{2,4},{3,5},{4,6},{5,7},{14,8},{15,9},{8,1... | collective-permute-start | bytes 786440 | tf_op jit(solution)/shard_map/ppermute | solution.py:45
  493.0 29.2 %collective-permute-start.2 = (f32[256,256]{0,1:T(8,128)S(1)}, f32[256,256]{0,1:T(8,128)S(1)}, u32[]{:S(2)}, u32[]{:S(2)}) collective-permute-start(f32[256,256]{0,1:T(8,128)S(1)} %copy.12), channel_id=1, source_target_pairs={{7,0},{0,1},{1,2},{2,3},{3,4},{4,5},{5,6},{6,7},{15,8},{8,9},{9,10... | collective-permute-start | bytes 786440 | tf_op jit(solution)/shard_map/ppermute | solution.py:45
  613.4 21.1 %collective-permute-start.5 = (f32[256,256]{0,1:T(8,128)S(1)}, f32[256,256]{0,1:T(8,128)S(1)}, u32[]{:S(2)}, u32[]{:S(2)}) collective-permute-start(f32[256,256]{0,1:T(8,128)S(1)} %copy.13), channel_id=1, source_target_pairs={{21,0},{22,1},{23,2},{16,3},{17,4},{18,5},{19,6},{20,7},{29,8},{30... | collective-permute-start | bytes 786440 | tf_op jit(solution)/shard_map/ppermute | solution.py:45
  614.6 19.9 %collective-permute-start.6 = (f32[256,256]{0,1:T(8,128)S(1)}, f32[256,256]{0,1:T(8,128)S(1)}, u32[]{:S(2)}, u32[]{:S(2)}) collective-permute-start(f32[256,256]{0,1:T(8,128)S(1)} %copy.14), channel_id=1, source_target_pairs={{22,0},{23,1},{16,2},{17,3},{18,4},{19,5},{20,6},{21,7},{30,8},{31... | collective-permute-start | bytes 786440 | tf_op jit(solution)/shard_map/ppermute | solution.py:45
  616.3 21.2 %copy-start.4 = (f32[2048,256]{1,0:T(8,128)S(1)}, f32[2048,256]{1,0:T(8,128)}, u32[]{:S(2)}) copy-start(f32[2048,256]{1,0:T(8,128)} %reduce-scatter.6.cloned.1.call-done) | copy-start | bytes 6291460
  616.3 19.6 %collective-permute-start.7 = (f32[256,256]{0,1:T(8,128)}, f32[256,256]{0,1:T(8,128)S(1)}, u32[]{:S(2)}, u32[]{:S(2)}) collective-permute-start(f32[256,256]{0,1:T(8,128)} %copy.15), channel_id=1, source_target_pairs={{23,0},{16,1},{17,2},{18,3},{19,4},{20,5},{21,6},{22,7},{31,8},{24... | collective-permute-start | bytes 786440 | tf_op jit(solution)/shard_map/ppermute | solution.py:45
Sparse Core Ops, SparseCore 0:
  75.4 107.5 reduce-scatter.3
  281.1 168.0 reduce-scatter.5
  490.4 121.6 reduce-scatter.7
